TPU v7x, 256 devices: a whole 4x4x8 slice. The times are simulated.
256 devices in a mesh: dp: 64 (over z, y, core), group: 4 (over x).
Axes of the slice: x: 4, y: 4, z: 8, core: 2. Of those that a mesh axis runs over, the one named last changes fastest.
Arguments:
- frames: bfloat16 [4, 36864, 2048], P('group', 'dp'), may hold values from -6 to 6
- lengths: int32 [4, 192], P('group', 'dp'), may hold values from 24 to 192, as said below
- destination: int32 [4, 192], P('group', 'dp'), may hold values from 0 to 63, as said below
- offsets: int32 [4, 192], P('group', 'dp'), may hold values from 0 to 360, as said below
- norm_gain: bfloat16 [2048], P(('dp', 'group')), may hold values from 0.099609375 to 1.8984375
- weight_in: bfloat16 [2048, 4096], P(('dp', 'group')), may hold values from -0.125 to 0.125
- depth_kernel: bfloat16 [2048, 32], P(('dp', 'group')), may hold values from -1 to 1
- post_gain: bfloat16 [2048], P(('dp', 'group')), may hold values from 0.099609375 to 1.8984375
- weight_out: bfloat16 [2048, 2048], P(('dp', 'group')), may hold values from -0.125 to 0.125
Outputs:
- mixed: bfloat16 [4, 24576, 2048], P('group', 'dp')
Inputs may be any that keep to these rules, and one draw needn't show every extreme that they name: `destination`: every device of a group sends exactly one utterance to itself, one to dp index + 1 and one to dp index - 1, both taken modulo 64, within its own group index. `lengths`: every device receives utterances with 384 frames in all; one utterance of each device's receipts has exactly 192 frames; in every group some device's slots are full. `offsets`: the utterances that one device receives lie back to back without gaps or intersection over its 384 rows.
All inputs are finite; a program needn't handle non-finite values.
Results may differ from a plain program's by a relative error of at most 0.0085.
Values may be sent and summed in bfloat16 or wider, within the bound.
A program may use at most 128 MiB of HBM per device.

v0:
```python
import jax
import jax.numpy as jnp
from jax import lax
from jax.sharding import PartitionSpec as P

D = 2048
KERNEL = 32
MAXLEN = 192
RCV_DEV = 384
IN_CHUNKS = 4
OUT_CHUNKS = 2
epsilon = 1e-05


def shifted(array, axis, by):
    peers = lax.axis_size(axis)
    return lax.ppermute(array, axis, [(i, (i + by) % peers) for i in range(peers)])


def layer_norm(values, scale_gain):
    center = values - jnp.mean(values, axis=-1, keepdims=True)
    spread = jnp.mean(center * center, axis=-1, keepdims=True)
    return center * lax.rsqrt(spread + epsilon) * scale_gain.astype(jnp.float32)


def depth_pass(gated_rows, segment, kernel_rows):
    row_count = gated_rows.shape[0]
    margin = KERNEL // 2
    padded = jnp.pad(gated_rows, ((margin, margin), (0, 0)))
    labels = jnp.pad(segment, (margin, margin), constant_values=-1)
    depthwise = jnp.zeros_like(gated_rows)
    for column in range(KERNEL):
        inside = (labels[column : column + row_count] == segment)[:, None]
        depthwise = (
            depthwise
            + jnp.where(inside, padded[column : column + row_count], 0.0) * kernel_rows[:, column]
        )
    return depthwise


def relocate(own_part, next_part, prev_part):
    from_prev = shifted((next_part[0], next_part[1]), "dp", 1)
    from_next = shifted((prev_part[0], prev_part[1]), "dp", -1)
    received = jnp.zeros((RCV_DEV + MAXLEN, D), jnp.bfloat16)
    segment = jnp.zeros((RCV_DEV,), jnp.int32)
    position = jnp.arange(RCV_DEV, dtype=jnp.int32)
    arrivals = (own_part, from_prev, from_next)
    for label_id in range(3):
        frame_rows, meta_data = arrivals[label_id]
        current = lax.dynamic_slice_in_dim(received, meta_data[1], MAXLEN, 0)
        received = lax.dynamic_update_slice_in_dim(received, current + frame_rows, meta_data[1], 0)
        inside = (position >= meta_data[1]) & (position < meta_data[1] + meta_data[0])
        segment = jnp.where(inside, label_id + 1, segment)
    return (received[:RCV_DEV], segment)


def shards(
    frames, lengths, destination, offsets, norm_gain, weight_in, depth_kernel, post_gain, weight_out
):
    axes = ("dp", "group")
    small = jnp.concatenate(
        [norm_gain.reshape(-1, 1), post_gain.reshape(-1, 1), depth_kernel], axis=1
    )
    width = D // IN_CHUNKS
    in_parts = []
    for c in range(IN_CHUNKS):
        columns = [
            weight_in[:, c * width : (c + 1) * width],
            weight_in[:, D + c * width : D + (c + 1) * width],
        ]
        if c == 0:
            columns.append(small)
        in_parts.append(lax.all_gather(jnp.concatenate(columns, axis=1), axes, axis=0, tiled=True))
    small_all = in_parts[0][:, 2 * width :]
    in_parts[0] = in_parts[0][:, : 2 * width]
    out_width = D // OUT_CHUNKS
    out_parts = [
        lax.all_gather(weight_out[:, m * out_width : (m + 1) * out_width], axes, axis=0, tiled=True)
        for m in range(OUT_CHUNKS)
    ]
    norm_full = small_all[:, 0]
    post_full = small_all[:, 1]
    kernel_full = small_all[:, 2:].astype(jnp.float32)
    dp_count = lax.axis_size("dp")
    my_index = lax.axis_index("dp")
    local_frames = frames[0]
    lengths_here = lengths[0]
    dest_here = destination[0]
    offsets_here = offsets[0]
    starts = jnp.cumsum(lengths_here) - lengths_here
    relative = (dest_here - my_index) % dp_count
    slot_ids = jnp.arange(3, dtype=jnp.int32)

    def pick_entry(values, which):
        return jnp.sum(jnp.where(slot_ids == which, values, 0))

    def slot_of(code):
        return jnp.sum(jnp.where(relative == code, slot_ids, 0))

    chosen = (slot_of(0), slot_of(1), slot_of(dp_count - 1))

    def cut_utterance(source_rows, which):
        start_row = pick_entry(starts, which)
        live_count = pick_entry(lengths_here, which)
        frame_rows = lax.dynamic_slice_in_dim(source_rows, start_row, MAXLEN, 0)
        keep_rows = jnp.arange(MAXLEN, dtype=jnp.int32) < live_count
        kept = jnp.where(keep_rows[:, None], frame_rows, jnp.zeros_like(frame_rows))
        return (kept, jnp.stack([live_count, pick_entry(offsets_here, which)]))

    received, segment = relocate(
        cut_utterance(local_frames, chosen[0]),
        cut_utterance(local_frames, chosen[1]),
        cut_utterance(local_frames, chosen[2]),
    )
    source = received.astype(jnp.float32)
    normed = layer_norm(source, norm_full).astype(jnp.bfloat16)
    pieces = []
    for c in range(IN_CHUNKS):
        projected = jnp.dot(normed, in_parts[c], preferred_element_type=jnp.float32)
        gated = projected[:, :width] * jax.nn.sigmoid(projected[:, width:])
        pieces.append(depth_pass(gated, segment, kernel_full[c * width : (c + 1) * width]))
    depthwise = jnp.concatenate(pieces, axis=1)
    normed_post = layer_norm(depthwise, post_full)
    active = (normed_post * jax.nn.sigmoid(normed_post)).astype(jnp.bfloat16)
    outs = []
    for m in range(OUT_CHUNKS):
        mixed = source[:, m * out_width : (m + 1) * out_width] + jnp.dot(
            active, out_parts[m], preferred_element_type=jnp.float32
        )
        outs.append(mixed.astype(jnp.bfloat16))
    return jnp.concatenate(outs, axis=1)[None]


def solution(mesh):
    placed = (
        P("group", "dp", None),
        P("group", "dp"),
        P("group", "dp"),
        P("group", "dp"),
        P(("dp", "group")),
        P(("dp", "group"), None),
        P(("dp", "group"), None),
        P(("dp", "group")),
        P(("dp", "group"), None),
    )
    return jax.shard_map(
        shards, mesh=mesh, in_specs=placed, out_specs=P("group", "dp", None), check_vma=False
    )
```

profile of v0, /device:TPU:1, one launch (start us, length us, event | category | flops | bytes accessed | tf_op | source)
XLA Modules:
  0.0 724.6 jit_solution(8807620519260074038)
XLA Ops:
  6.5 0.8 fusion.216
  7.4 0.7 copy.12
  8.9 1.4 concatenate.18
  12.5 1.3 fusion.217
  13.9 0.8 reduce-window.9
  14.7 1.4 fusion.201
  16.1 3.3 select_reduce_fusion
  25.7 1.3 iota_compare_fusion.6
  27.0 3.5 bitcast_select_fusion
  30.6 2.7 collective-permute-start.1
  33.2 2.6 fusion.205
  35.8 2.6 pad_add_fusion
  39.1 6.0 collective-permute-start.2
  48.5 4.0 dynamic_update_slice.9
  56.2 1.9 select_select_fusion
  62.2 1.4 dynamic-slice_add_fusion.1
  63.6 4.0 dynamic_update_slice.10
  67.7 1.4 dynamic-slice_add_fusion
  69.1 4.6 dynamic_update_slice.11
  74.0 2.0 slice_convert_fusion
  76.6 54.1 %all-gather.7.cloned.1.call-done = bf16[2048,1058]{1,0:T(8,128)(2,1)} async-done(((bf16[8,1058]{1,0:T(8,128)(2,1)}), bf16[2048,1058]{1,0:T(8,128)(2,1)}) %all-gather.7.cloned.1.call-update) | async-done | bytes 4333584 | tf_op jit(solution)/shard_map/all_gather | solution.py:73
  130.7 1.2 slice_convert_fusion.1
  132.0 3.2 slice_reduce_fusion.122
  135.2 2.6 slice_reduce_fusion.126
  137.8 2.7 slice_reduce_fusion.125
  140.5 3.2 slice_reduce_fusion.124
  143.7 2.8 slice_reduce_fusion.127
  146.5 3.3 slice_reduce_fusion.123
  150.3 1.9 fusion
  152.2 2.6 slice_reduce_fusion.121
  154.8 1.1 fusion.19
  155.9 91.0 %all-gather.9.cloned.1.call-done = bf16[2048,1024]{1,0:T(8,128)(2,1)} async-done(((bf16[8,1024]{1,0:T(8,128)(2,1)}), bf16[2048,1024]{1,0:T(8,128)(2,1)}) %all-gather.9.cloned.1.call-update) | async-done | bytes 4194320 | tf_op jit(solution)/shard_map/all_gather | solution.py:73
  246.9 4.1 fusion.211
  250.9 1.1 fusion.15
  252.0 111.0 %all-gather.11.cloned.1.call-done = bf16[2048,1024]{1,0:T(8,128)(2,1)} async-done(((bf16[8,1024]{1,0:T(8,128)(2,1)}), bf16[2048,1024]{1,0:T(8,128)(2,1)}) %all-gather.11.cloned.1.call-update) | async-done | bytes 4194320 | tf_op jit(solution)/shard_map/all_gather | solution.py:73
  363.0 4.1 fusion.210
  367.3 111.7 %all-gather.13.cloned.1.call-done = bf16[2048,1024]{1,0:T(8,128)(2,1)} async-done(((bf16[8,1024]{1,0:T(8,128)(2,1)}), bf16[2048,1024]{1,0:T(8,128)(2,1)}) %all-gather.13.cloned.1.call-update) | async-done | bytes 4194320 | tf_op jit(solution)/shard_map/all_gather | solution.py:73
  479.1 4.3 fusion.209
  484.1 6.0 fusion.213
  490.3 6.1 fusion.212
  496.4 5.3 fusion.214
  501.8 5.3 fusion.215
  507.6 2.7 multiply_convert_fusion
  510.3 84.7 %all-gather.17.cloned.1.call-done = bf16[2048,1024]{1,0:T(8,128)(2,1)} async-done(((bf16[8,1024]{1,0:T(8,128)(2,1)}), bf16[2048,1024]{1,0:T(8,128)(2,1)}) %all-gather.17.cloned.1.call-update) | async-done | bytes 4194320 | tf_op jit(solution)/shard_map/all_gather | solution.py:78
  595.0 5.6 fusion.220
  600.6 110.4 %all-gather.15.cloned.1.call-done = bf16[2048,1024]{1,0:T(8,128)(2,1)} async-done(((bf16[8,1024]{1,0:T(8,128)(2,1)}), bf16[2048,1024]{1,0:T(8,128)(2,1)}) %all-gather.15.cloned.1.call-update) | async-done | bytes 4194320 | tf_op jit(solution)/shard_map/all_gather | solution.py:78
  711.0 5.2 fusion.3
  716.2 1.3 maximum_bitcast_fusion
  (133 shorter events, 8.7 us)
Async XLA Ops:
  6.5 26.7 %copy-start.43 = (s32[1,3]{1,0:T(1,128)S(1)}, s32[1,3]{1,0:T(1,128)}, u32[]{:S(2)}) copy-start(s32[1,3]{1,0:T(1,128)} %param.12) | copy-start | bytes 40
  6.5 124.2 %all-gather.7.cloned.1.call-start = ((), (), s32[]{:S(2)}) async-start(), calls=%async_computation | async-start | bytes 4737024 | tf_op jit(solution)/shard_map/all_gather | solution.py:73
  10.2 236.6 %all-gather.9.cloned.1.call-start = ((), (), s32[]{:S(2)}) async-start(), calls=%async_computation.1 | async-start | bytes 4210688 | tf_op jit(solution)/shard_map/all_gather | solution.py:73
  11.0 352.0 %all-gather.11.cloned.1.call-start = ((), (), s32[]{:S(2)}) async-start(), calls=%async_computation.2 | async-start | bytes 4210688 | tf_op jit(solution)/shard_map/all_gather | solution.py:73
  11.7 467.3 %all-gather.13.cloned.1.call-start = ((), (), s32[]{:S(2)}) async-start(), calls=%async_computation.3 | async-start | bytes 4210688 | tf_op jit(solution)/shard_map/all_gather | solution.py:73
  12.4 582.6 %all-gather.17.cloned.1.call-start = ((), (), s32[]{:S(2)}) async-start(), calls=%async_computation.5 | async-start | bytes 4210688 | tf_op jit(solution)/shard_map/all_gather | solution.py:78
  13.8 697.2 %all-gather.15.cloned.1.call-start = ((), (), s32[]{:S(2)}) async-start(), calls=%async_computation.4 | async-start | bytes 4210688 | tf_op jit(solution)/shard_map/all_gather | solution.py:78
  30.6 31.6 %collective-permute-start.1 = (bf16[192,2048]{1,0:T(8,128)(2,1)}, bf16[192,2048]{1,0:T(8,128)(2,1)}, u32[]{:S(2)}, u32[]{:S(2)}) collective-permute-start(bf16[192,2048]{1,0:T(8,128)(2,1)} %get-tuple-element.159), channel_id=1, source_target_pairs={{0,4},{4,8},{8,12},{12,16},{16,20},{20,24},{24,28},{28,32},{32,36}... | collective-permute-start | bytes 2359304 | tf_op jit(solution)/shard_map/ppermute | solution.py:17
  38.4 16.1 %collective-permute-start = (s32[2]{0:T(128)S(1)}, s32[2]{0:T(128)S(1)}, u32[]{:S(2)}, u32[]{:S(2)}) collective-permute-start(s32[2]{0:T(128)S(1)} %get-tuple-element.205), channel_id=1, source_target_pairs={{0,4},{4,8},{8,12},{12,16},{16,20},{20,24},{24,28},{28,32},{32,36}... | collective-permute-start | bytes 32 | tf_op jit(solution)/shard_map/ppermute | solution.py:17
  38.4 29.2 %collective-permute-start.3 = (bf16[192,2048]{1,0:T(8,128)(2,1)}, bf16[192,2048]{1,0:T(8,128)(2,1)}, u32[]{:S(2)}, u32[]{:S(2)}) collective-permute-start(bf16[192,2048]{1,0:T(8,128)(2,1)} %get-tuple-element.157), channel_id=1, source_target_pairs={{0,252},{4,0},{8,4},{12,8},{16,12},{20,16},{24,20},{28,24},{32,28}... | collective-permute-start | bytes 2359304 | tf_op jit(solution)/shard_map/ppermute | solution.py:17
  39.1 13.4 %collective-permute-start.2 = (s32[2]{0:T(128)S(1)}, s32[2]{0:T(128)S(1)}, u32[]{:S(2)}, u32[]{:S(2)}) collective-permute-start(s32[2]{0:T(128)S(1)} %get-tuple-element.206), channel_id=1, source_target_pairs={{0,252},{4,0},{8,4},{12,8},{16,12},{20,16},{24,20},{28,24},{32,28}... | collective-permute-start | bytes 32 | tf_op jit(solution)/shard_map/ppermute | solution.py:17
  76.0 287.0 %copy-start.41 = (f32[384]{0:T(512)}, f32[384]{0:T(512)S(1)}, u32[]{:S(2)}) copy-start(f32[384]{0:T(512)S(1)} %broadcast_multiply_fusion) | copy-start | bytes 4612
  76.6 286.4 %copy-start.42 = (f32[384]{0:T(512)}, f32[384]{0:T(512)S(1)}, u32[]{:S(2)}) copy-start(f32[384]{0:T(512)S(1)} %add_rsqrt_fusion.1) | copy-start | bytes 4612
  140.5 9.3 %slice-start = ((s8[4718592]{0:T(1024)(128)(4,1)}), s8[4194304]{0:T(1024)(128)(4,1)S(1)}, s32[]{:S(2)}) async-start(s8[4718592]{0:T(1024)(128)(4,1)} %bitcast.63), calls=%async_computation.6 | async-start | bytes 8388608
  143.7 6.1 slice-start.1
  479.0 4.9 copy-start.12
  479.0 4.9 copy-start.13
  479.0 4.9 copy-start.14
  479.0 4.9 copy-start.15
  479.1 4.9 copy-start.16
  479.1 4.9 copy-start.17
  479.1 4.9 copy-start.18
  479.1 4.9 copy-start.19
  479.1 4.9 copy-start.20
  483.4 6.7 copy-start.1
  483.4 6.7 copy-start.3
  483.4 6.7 copy-start.4
  483.5 6.7 copy-start.5
  483.5 6.7 copy-start.6
  483.5 6.7 copy-start.7
  483.5 6.7 copy-start.22
  483.5 6.7 copy-start.23
  483.5 6.7 copy-start.24
  483.5 6.7 copy-start.25
  483.5 6.7 copy-start.26
  483.5 6.7 copy-start.27
  483.5 6.7 copy-start.28
  483.6 6.7 copy-start.29
  483.6 6.7 copy-start.32
  483.6 6.7 copy-start.33
  483.6 6.7 copy-start.34
  483.6 6.7 copy-start.35
  483.6 6.7 copy-start.36
  483.6 6.7 copy-start.37
  483.6 6.7 copy-start.38
  483.6 6.7 copy-start.39
  483.6 6.7 copy-start.40
  510.3 200.7 %copy-start = (f32[384,2048]{1,0:T(8,128)S(1)}, f32[384,2048]{1,0:T(8,128)}, u32[]{:S(2)}) copy-start(f32[384,2048]{1,0:T(8,128)} %slice_convert_fusion) | copy-start | bytes 9437188
  (8 other events, 39.3 us)
Sparse Core Ops, SparseCore 0:
  11.1 119.5 all-gather.6
  134.4 112.3 all-gather.8
  250.6 112.3 all-gather.10
  366.6 112.3 all-gather.12
  482.6 112.3 all-gather.16
  598.6 112.3 all-gather.14
where the time goes:
time: 730 us; the launch traced here: 725 us
  waiting for transfers between devices  563 us (77%)
  other arithmetic  57.6 us (8%)
  local copies, waits for them, and re-layouts  39.8 us (5%)
  between operations  29.5 us (4%)
  matrix products  25.1 us (3%)
  starting transfers between devices  9.56 us (1%)
    all_gather x4, waiting for transfers between devices, shards(): lax.all_gather(jnp.concatenate(columns, axis=1), axes, axis=0, tiled=True)  368 us
    all_gather x2, waiting for transfers between devices, shards(): lax.all_gather(weight_out[:, m * out_width:(m + 1) * out_width], axes, ax...  195 us
    reduce_sum x5, other arithmetic, layer_norm(): center = values - jnp.mean(values, axis=-1, keepdims=True)  23.1 us
    slice x7, local copies, waits for them, and re-layouts, depth_pass(): kernel_rows[:, column]  20.4 us
  transfers between devices with their start and end apart: 10, of which 6 were waited for; matrix products, arithmetic and copies ran while one was open for 15% of the time, Pallas kernels for 0%

commit v1 on v0

--- a/solution.py
+++ b/solution.py
@@ -70,7 +70,14 @@
         ]
         if c == 0:
             columns.append(small)
-        in_parts.append(lax.all_gather(jnp.concatenate(columns, axis=1), axes, axis=0, tiled=True))
+
+        def get_knots(load, bus_axis):
+            return jnp.concatenate(
+                lax.all_to_all(jnp.stack([load] * lax.axis_size(bus_axis), 0), bus_axis, 0, 0),
+                axis=0,
+            )
+
+        in_parts.append(get_knots(jnp.concatenate(columns, axis=1), axes))
     small_all = in_parts[0][:, 2 * width :]
     in_parts[0] = in_parts[0][:, : 2 * width]
     out_width = D // OUT_CHUNKS

time: 730 us -> 589 us (0.81)
  the two profiles are of different devices: /device:TPU:1 before, /device:TPU:6 now
where the time goes in v1:
time: 589 us; the launch traced here: 579 us
  waiting for transfers between devices  372 us (63%)
  other arithmetic  53.5 us (9%)
  starting transfers between devices  50.7 us (9%)
  local copies, waits for them, and re-layouts  46.3 us (8%)
  between operations  29.8 us (5%)
  matrix products  27.3 us (5%)
    all_to_all x4, waiting for transfers between devices, get_knots(): lax.all_to_all(jnp.stack([load] * lax.axis_size(bus_axis), 0), bus_axis,...  290 us
    ppermute x4, waiting for transfers between devices, shifted(): lax.ppermute(array, axis, [(i, (i + by) % peers) for i in range(peers)])  81.9 us
    all_to_all x4, starting transfers between devices, get_knots(): lax.all_to_all(jnp.stack([load] * lax.axis_size(bus_axis), 0), bus_axis,...  43.4 us
    reduce_sum x5, other arithmetic, layer_norm(): center = values - jnp.mean(values, axis=-1, keepdims=True)  23.1 us
    slice x7, local copies, waits for them, and re-layouts, depth_pass(): kernel_rows[:, column]  20.3 us
    dot_general x4, matrix products, shards(): projected = jnp.dot(normed, in_parts[c], preferred_element_type=jnp.float32)  16.4 us
    dynamic_update_slice x3, local copies, waits for them, and re-layouts, relocate(): lax.dynamic_update_slice_in_dim(received, current + frame_rows, meta_data...  12.5 us
  transfers between devices with their start and end apart: 10, of which 5 were waited for; matrix products, arithmetic and copies ran while one was open for 19% of the time, Pallas kernels for 0%

profile of v1, /device:TPU:6, one launch (start us, length us, event | category | flops | bytes accessed | tf_op | source)
XLA Modules:
  0.0 579.2 jit_solution(16900344370729472405)
XLA Ops:
  7.4 2.5 stack.27
  9.8 15.6 %all-to-all-start.1 = ((bf16[256,8,1024]{2,1,0:T(8,128)(2,1)}), bf16[256,8,1024]{2,1,0:T(8,128)(2,1)}, u32[]{:S(2)}, u32[]{:S(2)}) async-start(bf16[256,8,1024]{2,1,0:T(8,128)(2,1)} %stack.27), calls=%async_computation.1 | async-start | bytes 8388608 | tf_op jit(solution)/shard_map/all_to_all | solution.py:76
  25.5 95.7 %all-to-all-done.1 = bf16[256,8,1024]{2,1,0:T(8,128)(2,1)} async-done(((bf16[256,8,1024]{2,1,0:T(8,128)(2,1)}), bf16[256,8,1024]{2,1,0:T(8,128)(2,1)}, u32[]{:S(2)}, u32[]{:S(2)}) %all-to-all-start.1) | async-done | bytes 4194336 | tf_op jit(solution)/shard_map/all_to_all | solution.py:76
  121.2 2.5 stack.28
  123.7 9.2 %all-to-all-start.2 = ((bf16[256,8,1024]{2,1,0:T(8,128)(2,1)}), bf16[256,8,1024]{2,1,0:T(8,128)(2,1)}, u32[]{:S(2)}, u32[]{:S(2)}) async-start(bf16[256,8,1024]{2,1,0:T(8,128)(2,1)} %stack.28), calls=%async_computation.2 | async-start | bytes 8388608 | tf_op jit(solution)/shard_map/all_to_all | solution.py:76
  133.2 95.4 %all-to-all-done.2 = bf16[256,8,1024]{2,1,0:T(8,128)(2,1)} async-done(((bf16[256,8,1024]{2,1,0:T(8,128)(2,1)}), bf16[256,8,1024]{2,1,0:T(8,128)(2,1)}, u32[]{:S(2)}, u32[]{:S(2)}) %all-to-all-start.2) | async-done | bytes 4194336 | tf_op jit(solution)/shard_map/all_to_all | solution.py:76
  228.6 2.5 stack.26
  231.2 9.1 %all-to-all-start = ((bf16[256,8,1058]{2,1,0:T(8,128)(2,1)}), bf16[256,8,1058]{2,1,0:T(8,128)(2,1)}, u32[]{:S(2)}, u32[]{:S(2)}) async-start(bf16[256,8,1058]{2,1,0:T(8,128)(2,1)} %stack.26), calls=%async_computation | async-start | bytes 9437184 | tf_op jit(solution)/shard_map/all_to_all | solution.py:76
  242.0 2.7 select_reduce_fusion
  251.2 1.3 iota_compare_fusion.6
  252.5 98.5 %all-to-all-done = bf16[256,8,1058]{2,1,0:T(8,128)(2,1)} async-done(((bf16[256,8,1058]{2,1,0:T(8,128)(2,1)}), bf16[256,8,1058]{2,1,0:T(8,128)(2,1)}, u32[]{:S(2)}, u32[]{:S(2)}) %all-to-all-start) | async-done | bytes 4333600 | tf_op jit(solution)/shard_map/all_to_all | solution.py:76
  351.0 2.6 stack.29
  353.6 9.4 %all-to-all-start.3 = ((bf16[256,8,1024]{2,1,0:T(8,128)(2,1)}), bf16[256,8,1024]{2,1,0:T(8,128)(2,1)}, u32[]{:S(2)}, u32[]{:S(2)}) async-start(bf16[256,8,1024]{2,1,0:T(8,128)(2,1)} %stack.29), calls=%async_computation.3 | async-start | bytes 8388608 | tf_op jit(solution)/shard_map/all_to_all | solution.py:76
  363.1 1.9 bitcast_select_fusion
  365.2 2.7 fusion.211
  367.8 2.6 pad_add_fusion
  370.4 1.5 collective-permute-start
  371.9 5.0 collective-permute-start.3
  380.8 4.0 dynamic_update_slice.9
  384.9 77.2 %collective-permute-done.2 = s32[2]{0:T(128)S(1)} collective-permute-done((s32[2]{0:T(128)S(1)}, s32[2]{0:T(128)S(1)}, u32[]{:S(2)}, u32[]{:S(2)}) %collective-permute-start.2) | collective-permute-done | bytes 40 | tf_op jit(solution)/shard_map/ppermute | solution.py:17
  464.0 4.7 collective-permute-done
  470.4 1.8 select_select_fusion
  476.2 1.4 dynamic-slice_add_fusion.1
  477.7 4.0 dynamic_update_slice.10
  481.7 1.4 dynamic-slice_add_fusion
  483.2 4.4 dynamic_update_slice.11
  488.4 2.0 slice_convert_fusion
  490.5 1.8 convert_reduce_fusion.1
  492.3 1.3 slice_convert_fusion.1
  493.5 3.2 slice_reduce_fusion.122
  496.7 2.6 slice_reduce_fusion.126
  499.3 2.7 slice_reduce_fusion.125
  502.0 3.2 slice_reduce_fusion.124
  505.2 2.8 slice_reduce_fusion.127
  508.0 3.3 slice_reduce_fusion.123
  511.3 4.0 fusion
  515.3 2.6 slice_reduce_fusion.121
  519.0 4.0 fusion.6
  524.1 4.0 fusion.4
  528.6 4.4 fusion.2
  533.5 6.1 %fusion.216 = (f32[384]{0:T(512)S(1)}, f32[384,512]{1,0:T(8,128)S(1)}) fusion(f32[512]{0:T(512)S(1)} %copy-done.11, pred[384]{0:T(512)(128)(4,1)S(1)} %get-tuple-element.200, f32[512]{0:T(512)S(1)} %copy-done.12, pred[384]{0:T(512)(128)(4,1)S(1)} %get-tuple-element.171, f32[512]{0:T(512)S(1)} %copy-done.13, pred[384]{0:T(512)(128)(4,1)S(1)} %get-tuple-element.172, ...), kind=kLoop, calls=%fused_computation.499 | loop fusion | flops 18677376 | bytes 1651840 | tf_op jit(solution)/shard_map/reduce_sum | solution.py:21
  539.9 6.1 %fusion.215 = (f32[384]{0:T(512)S(1)}, f32[384,512]{1,0:T(8,128)S(1)}) fusion(f32[512]{0:T(512)S(1)} %copy-done.24, pred[384]{0:T(512)(128)(4,1)S(1)} %get-tuple-element.200, f32[512]{0:T(512)S(1)} %copy-done.25, pred[384]{0:T(512)(128)(4,1)S(1)} %get-tuple-element.171, f32[512]{0:T(512)S(1)} %copy-done.26, pred[384]{0:T(512)(128)(4,1)S(1)} %get-tuple-element.172, ...), kind=kLoop, calls=%fused_computation.498 | loop fusion | flops 18677376 | bytes 1651840 | tf_op jit(solution)/shard_map/reduce_sum | solution.py:21
  546.0 5.3 fusion.217
  551.3 5.3 fusion.218
  557.1 2.7 multiply_convert_fusion
  559.8 5.8 fusion.223
  565.6 5.1 fusion.9
  570.7 1.3 maximum_bitcast_fusion
  (142 shorter events, 10.0 us)
Async XLA Ops:
  9.8 111.4 %all-to-all-start.1 = ((bf16[256,8,1024]{2,1,0:T(8,128)(2,1)}), bf16[256,8,1024]{2,1,0:T(8,128)(2,1)}, u32[]{:S(2)}, u32[]{:S(2)}) async-start(bf16[256,8,1024]{2,1,0:T(8,128)(2,1)} %stack.27), calls=%async_computation.1 | async-start | bytes 8388608 | tf_op jit(solution)/shard_map/all_to_all | solution.py:76
  123.6 9.3 %copy-start.46 = (bf16[8]{0:T(256)(128)(2,1)S(1)}, bf16[8]{0:T(256)(128)(2,1)}, u32[]{:S(2)}) copy-start(bf16[8]{0:T(256)(128)(2,1)} %param.13) | copy-start | bytes 52
  123.7 9.4 %copy-start.47 = (bf16[8]{0:T(256)(128)(2,1)S(1)}, bf16[8]{0:T(256)(128)(2,1)}, u32[]{:S(2)}) copy-start(bf16[8]{0:T(256)(128)(2,1)} %param.16) | copy-start | bytes 52
  123.7 9.5 %copy-start.44 = (bf16[8,32]{1,0:T(8,128)(2,1)S(1)}, bf16[8,32]{1,0:T(8,128)(2,1)}, u32[]{:S(2)}) copy-start(bf16[8,32]{1,0:T(8,128)(2,1)} %param.15) | copy-start | bytes 1540
  123.7 105.0 %all-to-all-start.2 = ((bf16[256,8,1024]{2,1,0:T(8,128)(2,1)}), bf16[256,8,1024]{2,1,0:T(8,128)(2,1)}, u32[]{:S(2)}, u32[]{:S(2)}) async-start(bf16[256,8,1024]{2,1,0:T(8,128)(2,1)} %stack.28), calls=%async_computation.2 | async-start | bytes 8388608 | tf_op jit(solution)/shard_map/all_to_all | solution.py:76
  231.2 9.2 %copy-start.4 = (bf16[8,2048]{1,0:T(8,128)(2,1)S(1)}, bf16[8,2048]{1,0:T(8,128)(2,1)}, u32[]{:S(2)}) copy-start(bf16[8,2048]{1,0:T(8,128)(2,1)} %param.17) | copy-start | bytes 98308
  231.2 9.9 %copy-start.50 = (s32[1,3]{1,0:T(1,128)S(1)}, s32[1,3]{1,0:T(1,128)}, u32[]{:S(2)}) copy-start(s32[1,3]{1,0:T(1,128)} %param.10) | copy-start | bytes 40
  231.2 10.1 %copy-start.48 = (s32[1,3]{1,0:T(1,128)S(1)}, s32[1,3]{1,0:T(1,128)}, u32[]{:S(2)}) copy-start(s32[1,3]{1,0:T(1,128)} %param.11) | copy-start | bytes 40
  231.2 119.8 %all-to-all-start = ((bf16[256,8,1058]{2,1,0:T(8,128)(2,1)}), bf16[256,8,1058]{2,1,0:T(8,128)(2,1)}, u32[]{:S(2)}, u32[]{:S(2)}) async-start(bf16[256,8,1058]{2,1,0:T(8,128)(2,1)} %stack.26), calls=%async_computation | async-start | bytes 9437184 | tf_op jit(solution)/shard_map/all_to_all | solution.py:76
  240.3 319.5 %all-gather.5.cloned.1.call-start = ((), (), s32[]{:S(2)}) async-start(), calls=%async_computation.5 | async-start | bytes 4210688 | tf_op jit(solution)/shard_map/all_gather | solution.py:85
  353.6 9.5 %copy-start.3 = (bf16[1,576,2048]{2,1,0:T(8,128)(2,1)S(1)}, bf16[1,576,2048]{2,1,0:T(8,128)(2,1)}, u32[]{:S(2)}) copy-start(bf16[1,576,2048]{2,1,0:T(8,128)(2,1)} %param.9) | copy-start | bytes 7077892
  353.6 174.8 %all-to-all-start.3 = ((bf16[256,8,1024]{2,1,0:T(8,128)(2,1)}), bf16[256,8,1024]{2,1,0:T(8,128)(2,1)}, u32[]{:S(2)}, u32[]{:S(2)}) async-start(bf16[256,8,1024]{2,1,0:T(8,128)(2,1)} %stack.29), calls=%async_computation.3 | async-start | bytes 8388608 | tf_op jit(solution)/shard_map/all_to_all | solution.py:76
  363.0 202.5 %all-gather.3.cloned.1.call-start = ((), (), s32[]{:S(2)}) async-start(), calls=%async_computation.4 | async-start | bytes 4210688 | tf_op jit(solution)/shard_map/all_gather | solution.py:85
  365.0 111.2 %collective-permute-start.1 = (bf16[192,2048]{1,0:T(8,128)(2,1)}, bf16[192,2048]{1,0:T(8,128)(2,1)}, u32[]{:S(2)}, u32[]{:S(2)}) collective-permute-start(bf16[192,2048]{1,0:T(8,128)(2,1)} %get-tuple-element.159), channel_id=1, source_target_pairs={{0,4},{4,8},{8,12},{12,16},{16,20},{20,24},{24,28},{28,32},{32,36}... | collective-permute-start | bytes 2359304 | tf_op jit(solution)/shard_map/ppermute | solution.py:17
  370.4 98.2 %collective-permute-start = (s32[2]{0:T(128)S(1)}, s32[2]{0:T(128)S(1)}, u32[]{:S(2)}, u32[]{:S(2)}) collective-permute-start(s32[2]{0:T(128)S(1)} %get-tuple-element.205), channel_id=1, source_target_pairs={{0,4},{4,8},{8,12},{12,16},{16,20},{20,24},{24,28},{28,32},{32,36}... | collective-permute-start | bytes 32 | tf_op jit(solution)/shard_map/ppermute | solution.py:17
  371.9 109.9 %collective-permute-start.3 = (bf16[192,2048]{1,0:T(8,128)(2,1)}, bf16[192,2048]{1,0:T(8,128)(2,1)}, u32[]{:S(2)}, u32[]{:S(2)}) collective-permute-start(bf16[192,2048]{1,0:T(8,128)(2,1)} %get-tuple-element.157), channel_id=1, source_target_pairs={{0,252},{4,0},{8,4},{12,8},{16,12},{20,16},{24,20},{28,24},{32,28}... | collective-permute-start | bytes 2359304 | tf_op jit(solution)/shard_map/ppermute | solution.py:17
  376.9 85.2 %collective-permute-start.2 = (s32[2]{0:T(128)S(1)}, s32[2]{0:T(128)S(1)}, u32[]{:S(2)}, u32[]{:S(2)}) collective-permute-start(s32[2]{0:T(128)S(1)} %get-tuple-element.206), channel_id=1, source_target_pairs={{0,252},{4,0},{8,4},{12,8},{16,12},{20,16},{24,20},{28,24},{32,28}... | collective-permute-start | bytes 32 | tf_op jit(solution)/shard_map/ppermute | solution.py:17
  487.9 36.2 %copy-start.43 = (f32[384]{0:T(512)}, f32[384]{0:T(512)S(1)}, u32[]{:S(2)}) copy-start(f32[384]{0:T(512)S(1)} %broadcast_multiply_fusion) | copy-start | bytes 4612
  488.4 35.7 %copy-start.45 = (f32[384]{0:T(512)}, f32[384]{0:T(512)S(1)}, u32[]{:S(2)}) copy-start(f32[384]{0:T(512)S(1)} %add_rsqrt_fusion.1) | copy-start | bytes 4612
  528.4 5.0 copy-start.2
  528.4 5.0 copy-start.10
  528.4 5.0 copy-start.11
  528.4 5.0 copy-start.12
  528.4 5.0 copy-start.13
  532.9 6.7 %copy-start.1 = (f32[384,512]{1,0:T(8,128)S(1)}, f32[384,512]{1,0:T(8,128)}, u32[]{:S(2)}) copy-start(f32[384,512]{1,0:T(8,128)} %fusion.21) | copy-start | bytes 2359300
  532.9 6.7 %copy-start.5 = (f32[512]{0:T(512)S(1)}, f32[512]{0:T(512)}, u32[]{:S(2)}) copy-start(f32[512]{0:T(512)} %get-tuple-element.104) | copy-start | bytes 6148
  532.9 6.7 %copy-start.6 = (f32[512]{0:T(512)S(1)}, f32[512]{0:T(512)}, u32[]{:S(2)}) copy-start(f32[512]{0:T(512)} %get-tuple-element.105) | copy-start | bytes 6148
  533.0 6.7 %copy-start.7 = (f32[512]{0:T(512)S(1)}, f32[512]{0:T(512)}, u32[]{:S(2)}) copy-start(f32[512]{0:T(512)} %get-tuple-element.106) | copy-start | bytes 6148
  533.0 6.7 %copy-start.8 = (f32[512]{0:T(512)S(1)}, f32[512]{0:T(512)}, u32[]{:S(2)}) copy-start(f32[512]{0:T(512)} %get-tuple-element.107) | copy-start | bytes 6148
  533.0 6.7 %copy-start.9 = (f32[512]{0:T(512)S(1)}, f32[512]{0:T(512)}, u32[]{:S(2)}) copy-start(f32[512]{0:T(512)} %get-tuple-element.108) | copy-start | bytes 6148
  533.0 6.7 %copy-start.24 = (f32[512]{0:T(512)S(1)}, f32[512]{0:T(512)}, u32[]{:S(2)}) copy-start(f32[512]{0:T(512)} %get-tuple-element.75) | copy-start | bytes 6148
  533.0 6.7 %copy-start.25 = (f32[512]{0:T(512)S(1)}, f32[512]{0:T(512)}, u32[]{:S(2)}) copy-start(f32[512]{0:T(512)} %get-tuple-element.76) | copy-start | bytes 6148
  533.0 6.7 %copy-start.26 = (f32[512]{0:T(512)S(1)}, f32[512]{0:T(512)}, u32[]{:S(2)}) copy-start(f32[512]{0:T(512)} %get-tuple-element.77) | copy-start | bytes 6148
  533.0 6.7 %copy-start.27 = (f32[512]{0:T(512)S(1)}, f32[512]{0:T(512)}, u32[]{:S(2)}) copy-start(f32[512]{0:T(512)} %get-tuple-element.78) | copy-start | bytes 6148
  533.0 6.7 %copy-start.28 = (f32[512]{0:T(512)S(1)}, f32[512]{0:T(512)}, u32[]{:S(2)}) copy-start(f32[512]{0:T(512)} %get-tuple-element.79) | copy-start | bytes 6148
  533.0 6.7 %copy-start.29 = (f32[512]{0:T(512)S(1)}, f32[512]{0:T(512)}, u32[]{:S(2)}) copy-start(f32[512]{0:T(512)} %get-tuple-element.80) | copy-start | bytes 6148
  533.0 6.7 %copy-start.30 = (f32[512]{0:T(512)S(1)}, f32[512]{0:T(512)}, u32[]{:S(2)}) copy-start(f32[512]{0:T(512)} %get-tuple-element.81) | copy-start | bytes 6148
  533.1 6.7 %copy-start.31 = (f32[512]{0:T(512)S(1)}, f32[512]{0:T(512)}, u32[]{:S(2)}) copy-start(f32[512]{0:T(512)} %get-tuple-element.82) | copy-start | bytes 6148
  533.1 6.7 %copy-start.34 = (f32[512]{0:T(512)S(1)}, f32[512]{0:T(512)}, u32[]{:S(2)}) copy-start(f32[512]{0:T(512)} %get-tuple-element.84) | copy-start | bytes 6148
  533.1 6.7 %copy-start.35 = (f32[512]{0:T(512)S(1)}, f32[512]{0:T(512)}, u32[]{:S(2)}) copy-start(f32[512]{0:T(512)} %get-tuple-element.85) | copy-start | bytes 6148
  533.1 6.7 %copy-start.36 = (f32[512]{0:T(512)S(1)}, f32[512]{0:T(512)}, u32[]{:S(2)}) copy-start(f32[512]{0:T(512)} %get-tuple-element.86) | copy-start | bytes 6148
  533.1 6.7 %copy-start.37 = (f32[512]{0:T(512)S(1)}, f32[512]{0:T(512)}, u32[]{:S(2)}) copy-start(f32[512]{0:T(512)} %get-tuple-element.87) | copy-start | bytes 6148
  533.1 6.7 %copy-start.38 = (f32[512]{0:T(512)S(1)}, f32[512]{0:T(512)}, u32[]{:S(2)}) copy-start(f32[512]{0:T(512)} %get-tuple-element.88) | copy-start | bytes 6148
  533.1 6.7 %copy-start.39 = (f32[512]{0:T(512)S(1)}, f32[512]{0:T(512)}, u32[]{:S(2)}) copy-start(f32[512]{0:T(512)} %get-tuple-element.89) | copy-start | bytes 6148
  533.1 6.7 %copy-start.40 = (f32[512]{0:T(512)S(1)}, f32[512]{0:T(512)}, u32[]{:S(2)}) copy-start(f32[512]{0:T(512)} %get-tuple-element.90) | copy-start | bytes 6148
  533.1 6.7 %copy-start.41 = (f32[512]{0:T(512)S(1)}, f32[512]{0:T(512)}, u32[]{:S(2)}) copy-start(f32[512]{0:T(512)} %get-tuple-element.91) | copy-start | bytes 6148
  533.1 6.7 %copy-start.42 = (f32[512]{0:T(512)S(1)}, f32[512]{0:T(512)}, u32[]{:S(2)}) copy-start(f32[512]{0:T(512)} %get-tuple-element.92) | copy-start | bytes 6148
  559.8 5.8 %copy-start = (f32[384,2048]{1,0:T(8,128)S(1)}, f32[384,2048]{1,0:T(8,128)}, u32[]{:S(2)}) copy-start(f32[384,2048]{1,0:T(8,128)} %slice_convert_fusion) | copy-start | bytes 9437188
  (13 other events, 62.1 us)
Sparse Core Ops, SparseCore 0:
  244.8 123.3 all-gather.4
  377.6 118.0 all-gather.2
